TPU v7x, 32 devices: a whole 2x2x4 slice. The times are simulated.
32 devices in a mesh: band: 8 (over z, y), tok: 4 (over x, core).
Axes of the slice: x: 2, y: 2, z: 4, core: 2. Of those that a mesh axis runs over, the one named last changes fastest.
Arguments:
- pixels: bfloat16 [4, 8, 32, 256, 256], P('tok', None, 'band'), may hold values from -6 to 6
- wave_table: float32 [64], replicated, may hold values from 0.4 to 12
- wave_index: int32 [4, 8, 32], P('tok'), may hold values from 0 to 63
- patch_count: int32 [4, 8], P('tok', 'band'), may hold values from 49 to 256, as said below
- d_out: bfloat16 [4, 8, 256, 768], P('tok', 'band'), may hold values from -6 to 6
- gen_w: bfloat16 [196608, 128], P(('band', 'tok')), may hold values from -0.5 to 0.5
- gen_b: float32 [128, 768], replicated, may hold values from -0.25 to 0.25
- bias_token: float32 [128], replicated, may hold values from -6 to 6
- hyper_query: float32 [128, 128], replicated, may hold values from -1 to 1
- hyper_key: float32 [128, 128], replicated, may hold values from -1 to 1
- hyper_value: float32 [128, 128], replicated, may hold values from -0.5 to 0.5
- hyper_out: float32 [128, 128], replicated, may hold values from -0.5 to 0.5
- hyper_up: float32 [128, 2048], replicated, may hold values from -0.5 to 0.5
- hyper_down: float32 [2048, 128], replicated, may hold values from -0.125 to 0.125
- hyper_gain1: float32 [128], replicated, may hold values from 0.1 to 1.9
- hyper_gain2: float32 [128], replicated, may hold values from 0.1 to 1.9
- w_qkv: bfloat16 [768, 2304], P(None, 'tok'), may hold values from -0.21875 to 0.21875
- w_out: bfloat16 [768, 768], P(None, 'tok'), may hold values from -1.75 to 1.75
- w_up: bfloat16 [768, 3072], P(None, 'tok'), may hold values from -0.21875 to 0.21875
- w_down: bfloat16 [3072, 768], P('tok'), may hold values from -0.109375 to 0.109375
- ln1_gain: float32 [768], replicated, may hold values from 0.5 to 1.5
- ln2_gain: float32 [768], replicated, may hold values from 0.5 to 1.5
Outputs:
- layer_out: bfloat16 [4, 8, 256, 768], P('tok', 'band')
- pixel_grad: bfloat16 [4, 8, 32, 256, 256], P('tok', None, 'band')
- grad_gen_w: float32 [196608, 128], P(('band', 'tok'))
- grad_gen_b: float32 [128, 768], replicated
- grad_bias_token: float32 [128], replicated
- grad_hyper_query: float32 [128, 128], replicated
- grad_hyper_key: float32 [128, 128], replicated
- grad_hyper_value: float32 [128, 128], replicated
- grad_hyper_out: float32 [128, 128], replicated
- grad_hyper_up: float32 [128, 2048], replicated
- grad_hyper_down: float32 [2048, 128], replicated
- grad_hyper_gain1: float32 [128], replicated
- grad_hyper_gain2: float32 [128], replicated
- grad_w_qkv: float32 [768, 2304], P(None, ('band', 'tok'))
- grad_w_out: float32 [768, 768], P(None, ('band', 'tok'))
- grad_w_up: float32 [768, 3072], P(None, ('band', 'tok'))
- grad_w_down: float32 [3072, 768], P(('band', 'tok'))
- grad_ln1_gain: float32 [768], P(('band', 'tok'))
- grad_ln2_gain: float32 [768], P(('band', 'tok'))
Inputs may be any that keep to these rules, and one draw needn't show every extreme that they name: `patch_count`: each entry is 49, 196 or 256; every draw has an image with 49 and one with 256.
All inputs are finite; a program needn't handle non-finite values.
Results may differ from a plain program's by a relative error of at most 0.028.
Values may be sent and summed in bfloat16 or wider, within the bound.
A program may use at most 384 MiB of HBM per device.

v0:
```python
import math
import jax
import jax.numpy as jnp
from jax import lax
from jax.sharding import PartitionSpec as P

HD = 64
HHEADS = 4
EPS_BLOCK = 1e-06
EPS_HYPER = 1e-05
PRECISE = lax.Precision.HIGHEST


def layer_norm(values, scaling, epsilon):
    center = values - jnp.mean(values, axis=-1, keepdims=True)
    spread = jnp.mean(center * center, axis=-1, keepdims=True)
    return center * lax.rsqrt(spread + epsilon) * scaling


def block_norm(values, scaling):
    return layer_norm(values, scaling, EPS_BLOCK)


def exact_gelu(values):
    return jax.nn.gelu(values, approximate=False)


def wave_features(lengths, model_dim):
    middle = model_dim // 2
    angular = 1.0 / 10000.0 ** (jnp.arange(middle, dtype=jnp.float32) / middle)
    phases = (100.0 * lengths)[..., None] * angular
    return jnp.concatenate([jnp.sin(phases), jnp.cos(phases)], axis=-1)


def hyper_layer(features, params):
    (
        bias_token,
        hyper_query,
        hyper_key,
        hyper_value,
        hyper_out,
        hyper_up,
        hyper_down,
        hyper_gain1,
        hyper_gain2,
    ) = params
    images = features.shape[0]
    model_dim = features.shape[-1]
    head_size = model_dim // HHEADS
    tokens = jnp.concatenate(
        [features, jnp.broadcast_to(bias_token, (images, 1, model_dim))], axis=1
    )
    length = tokens.shape[1]
    queries = jnp.einsum("nsc,ce->nse", tokens, hyper_query, precision=PRECISE).reshape(
        images, length, HHEADS, head_size
    )
    keys_all = jnp.einsum("nsc,ce->nse", tokens, hyper_key, precision=PRECISE).reshape(
        images, length, HHEADS, head_size
    )
    values_all = jnp.einsum("nsc,ce->nse", tokens, hyper_value, precision=PRECISE).reshape(
        images, length, HHEADS, head_size
    )
    scores = jnp.einsum("nshe,nthe->nhst", queries, keys_all, precision=PRECISE) / math.sqrt(
        head_size
    )
    weights = jax.nn.softmax(scores, axis=-1)
    blended = jnp.einsum("nhst,nthe->nshe", weights, values_all, precision=PRECISE).reshape(
        images, length, model_dim
    )
    segment_one = layer_norm(
        tokens + jnp.einsum("nse,ef->nsf", blended, hyper_out, precision=PRECISE),
        hyper_gain1,
        EPS_HYPER,
    )
    expanded = jax.nn.gelu(
        jnp.einsum("nse,ef->nsf", segment_one, hyper_up, precision=PRECISE), approximate=False
    )
    second = layer_norm(
        segment_one + jnp.einsum("nsf,fe->nse", expanded, hyper_down, precision=PRECISE),
        hyper_gain2,
        EPS_HYPER,
    )
    return (second[:, :-1, :], second[:, -1, :])


def contract_rows(left_side, right_side):
    return lax.dot_general(
        left_side, right_side, (((0,), (0,)), ((), ())), preferred_element_type=jnp.float32
    )


def contract_cols(left_side, right_side):
    return lax.dot_general(
        left_side, right_side, (((1,), (1,)), ((), ())), preferred_element_type=jnp.float32
    )


def attention_scores(queries, keys_low, usable):
    head_size = queries.shape[-1]
    scores = jnp.einsum(
        "iqhe,ikhe->ihqk", queries, keys_low, preferred_element_type=jnp.float32
    ) / math.sqrt(head_size)
    return jnp.where(usable[:, None, None, :], scores, -1e30)


def block_forward(embedded, usable, weights_full, ln1_gain, ln2_gain):
    w_qkv_full, w_out_full, w_up_full, w_down_full = weights_full
    images, slot_count, model_dim = embedded.shape
    row_count = images * slot_count
    head_count = model_dim // HD
    flat_rows = embedded.reshape(row_count, model_dim)
    normed_one = block_norm(flat_rows, ln1_gain).astype(jnp.bfloat16)
    qkv_low = jnp.dot(normed_one, w_qkv_full, preferred_element_type=jnp.float32).astype(
        jnp.bfloat16
    )
    sections = qkv_low.reshape(images, slot_count, 3, head_count, HD)
    queries = sections[:, :, 0]
    keys_low = sections[:, :, 1]
    values_low = sections[:, :, 2]
    scores = attention_scores(queries, keys_low, usable)
    highest = jnp.max(scores, axis=-1, keepdims=True)
    lifted = jnp.exp(scores - highest)
    totals = jnp.sum(lifted, axis=-1, keepdims=True)
    attn_probs = (lifted / totals).astype(jnp.bfloat16)
    log_mass = highest + jnp.log(totals)
    attended = (
        jnp.einsum("ihqk,ikhe->iqhe", attn_probs, values_low, preferred_element_type=jnp.float32)
        .astype(jnp.bfloat16)
        .reshape(row_count, model_dim)
    )
    middle = flat_rows + jnp.dot(attended, w_out_full, preferred_element_type=jnp.float32)
    normed_two = block_norm(middle, ln2_gain).astype(jnp.bfloat16)
    hidden = jnp.dot(normed_two, w_up_full, preferred_element_type=jnp.float32)
    active = exact_gelu(hidden).astype(jnp.bfloat16)
    output = middle + jnp.dot(active, w_down_full, preferred_element_type=jnp.float32)
    return (
        flat_rows,
        normed_one,
        queries,
        keys_low,
        values_low,
        log_mass,
        attended,
        middle,
        normed_two,
        hidden,
        active,
        output,
    )


def block_backward(stored, usable, grad_rows, weights_full, ln1_gain, ln2_gain):
    (
        flat_rows,
        normed_one,
        queries,
        keys_low,
        values_low,
        log_mass,
        attended,
        middle,
        normed_two,
        hidden,
        active,
        output,
    ) = stored
    w_qkv_full, w_out_full, w_up_full, w_down_full = weights_full
    images, slot_count, head_count, head_size = queries.shape
    row_count, model_dim = flat_rows.shape
    grad_low = grad_rows.astype(jnp.bfloat16)
    grad_down = contract_rows(active, grad_low)
    d_active = contract_cols(grad_low, w_down_full)
    gelu_back = jax.vjp(exact_gelu, hidden)[1]
    d_hidden = gelu_back(d_active)[0].astype(jnp.bfloat16)
    grad_up_turned = contract_rows(d_hidden, normed_two)
    d_normed_two = contract_cols(d_hidden, w_up_full)
    norm_back_two = jax.vjp(block_norm, middle, ln2_gain)[1]
    d_middle_norm, grad_gain_two = norm_back_two(d_normed_two)
    d_middle = grad_rows + d_middle_norm
    d_middle_low = d_middle.astype(jnp.bfloat16)
    grad_out_turned = contract_rows(d_middle_low, attended)
    d_attended = (
        contract_cols(d_middle_low, w_out_full)
        .astype(jnp.bfloat16)
        .reshape(images, slot_count, head_count, head_size)
    )
    scores = attention_scores(queries, keys_low, usable)
    attn_float = jnp.exp(scores - log_mass)
    attn_probs = attn_float.astype(jnp.bfloat16)
    d_values = jnp.einsum(
        "ihqk,iqhe->ikhe", attn_probs, d_attended, preferred_element_type=jnp.float32
    ).astype(jnp.bfloat16)
    d_probs = jnp.einsum(
        "iqhe,ikhe->ihqk", d_attended, values_low, preferred_element_type=jnp.float32
    )
    d_scores = (
        attn_float * (d_probs - jnp.sum(attn_float * d_probs, axis=-1, keepdims=True))
    ).astype(jnp.bfloat16)
    d_queries = (
        jnp.einsum("ihqk,ikhe->iqhe", d_scores, keys_low, preferred_element_type=jnp.float32)
        / math.sqrt(head_size)
    ).astype(jnp.bfloat16)
    d_keys = (
        jnp.einsum("ihqk,iqhe->ikhe", d_scores, queries, preferred_element_type=jnp.float32)
        / math.sqrt(head_size)
    ).astype(jnp.bfloat16)
    d_qkv = jnp.stack([d_queries, d_keys, d_values], axis=2).reshape(row_count, 3 * model_dim)
    grad_qkv_turned = contract_rows(d_qkv, normed_one)
    d_normed_one = contract_cols(d_qkv, w_qkv_full)
    norm_back_one = jax.vjp(block_norm, flat_rows, ln1_gain)[1]
    d_flat, grad_gain_one = norm_back_one(d_normed_one)
    return (
        d_middle + d_flat,
        (grad_qkv_turned, grad_out_turned, grad_up_turned, grad_down, grad_gain_one, grad_gain_two),
    )


def body(
    pixels,
    wave_table,
    wave_index,
    patch_count,
    d_out,
    gen_w,
    gen_b,
    bias_token,
    hyper_query,
    hyper_key,
    hyper_value,
    hyper_out,
    hyper_up,
    hyper_down,
    hyper_gain1,
    hyper_gain2,
    w_qkv,
    w_out,
    w_up,
    w_down,
    ln1_gain,
    ln2_gain,
):
    group_images = pixels.shape[1]
    band_share = pixels.shape[2]
    slot_count = pixels.shape[3]
    pixel_count = pixels.shape[4]
    own_images = patch_count.shape[1]
    model_dim = w_out.shape[0]
    hyper_dim = gen_w.shape[1]
    all_bands = wave_index.shape[2]
    factor = 1.0 / math.sqrt(all_bands * pixel_count)
    band_place = lax.axis_index("band")
    hyper_params = (
        bias_token,
        hyper_query,
        hyper_key,
        hyper_value,
        hyper_out,
        hyper_up,
        hyper_down,
        hyper_gain1,
        hyper_gain2,
    )
    catalog = lax.broadcasted_iota(jnp.int32, (1, 1, wave_table.shape[0]), 2)
    picked = (wave_index[0][:, :, None] == catalog).astype(jnp.float32)
    lengths_all = jnp.sum(picked * wave_table, axis=-1)
    weights_full = (
        lax.all_gather(w_qkv, "tok", axis=1, tiled=True),
        lax.all_gather(w_out, "tok", axis=1, tiled=True),
        lax.all_gather(w_up, "tok", axis=1, tiled=True),
        lax.all_gather(w_down, "tok", axis=0, tiled=True),
    )
    hyper_input = wave_features(lengths_all, hyper_dim)

    def run_hyper(params):
        return hyper_layer(hyper_input, params)

    (band_feats, bias_feats), hyper_back = jax.vjp(run_hyper, hyper_params)
    band_low = (
        lax.dynamic_slice_in_dim(band_feats, band_place * band_share, band_share, 1)
        .astype(jnp.bfloat16)
        .reshape(-1, hyper_dim)
    )
    bias_own = lax.dynamic_slice_in_dim(bias_feats, band_place * own_images, own_images, 0)
    gen_full = lax.all_gather(gen_w, ("band", "tok"), axis=0, tiled=True)
    kernels = (contract_cols(band_low, gen_full) * factor).astype(jnp.bfloat16)
    kernel_grid = kernels.reshape(group_images, band_share, pixel_count, model_dim)
    pixel_part = pixels[0]
    product = jnp.einsum(
        "ibsp,ibpd->isd", pixel_part, kernel_grid, preferred_element_type=jnp.float32
    )
    convolved = lax.psum_scatter(
        product.reshape(own_images * slot_count * lax.axis_size("band"), model_dim).astype(
            jnp.bfloat16
        ),
        "band",
        scatter_dimension=0,
        tiled=True,
    ).astype(jnp.float32)
    bias_rows = jnp.dot(bias_own, gen_b, precision=PRECISE)
    embedded = convolved.reshape(own_images, slot_count, model_dim) + bias_rows[:, None, :]
    usable = lax.broadcasted_iota(jnp.int32, (own_images, slot_count), 1) < patch_count[0][:, None]
    stored = block_forward(embedded, usable, weights_full, ln1_gain, ln2_gain)
    row_mask = usable.reshape(-1, 1)
    layer_out = (
        jnp.where(row_mask, stored[-1], 0.0)
        .astype(jnp.bfloat16)
        .reshape(1, own_images, slot_count, model_dim)
    )
    stored = block_forward(
        lax.optimization_barrier(embedded), usable, weights_full, ln1_gain, ln2_gain
    )
    grad_rows = jnp.where(row_mask, d_out[0].reshape(-1, model_dim).astype(jnp.float32), 0.0)
    d_embed, block_terms = block_backward(
        stored, usable, grad_rows, weights_full, ln1_gain, ln2_gain
    )
    d_embed_low = d_embed.astype(jnp.bfloat16).reshape(own_images, slot_count, model_dim)
    d_bias = jnp.sum(d_embed.reshape(own_images, slot_count, model_dim), axis=1)
    d_bias_feat = jnp.dot(d_bias, gen_b.T, precision=PRECISE)
    grad_gen_b = jnp.dot(bias_own.T, d_bias, precision=PRECISE)
    d_gathered = lax.all_gather(d_embed_low, "band", axis=0, tiled=True)
    pixel_grad = jnp.einsum(
        "isd,ibpd->ibsp", d_gathered, kernel_grid, preferred_element_type=jnp.float32
    ).astype(jnp.bfloat16)[None]
    d_kernel = (
        jnp.einsum("ibsp,isd->ibpd", pixels[0], d_gathered, preferred_element_type=jnp.float32)
        .astype(jnp.bfloat16)
        .reshape(-1, pixel_count * model_dim)
    )
    d_band_local = jnp.dot(d_kernel, gen_full, preferred_element_type=jnp.float32) * factor
    grad_gen_w = lax.psum_scatter(
        contract_rows(d_kernel, band_low) * factor, ("band", "tok"), scatter_dimension=0, tiled=True
    )
    d_band_own = d_band_local.reshape(group_images, band_share, hyper_dim)
    d_band = lax.dynamic_update_slice_in_dim(
        jnp.zeros(band_feats.shape, jnp.float32), d_band_own, band_place * band_share, 1
    )
    d_bias_all = lax.dynamic_update_slice_in_dim(
        jnp.zeros(bias_feats.shape, jnp.float32), d_bias_feat, band_place * own_images, 0
    )
    (
        grad_token,
        grad_query,
        grad_key,
        grad_value,
        grad_mix,
        grad_expand,
        grad_shrink,
        grad_first_gain,
        grad_second_gain,
    ) = hyper_back((d_band, d_bias_all))[0]
    qkv_turned, out_turned, up_turned, grad_down, gain_one, gain_two = block_terms
    block_sums = (
        lax.psum_scatter(qkv_turned, ("band", "tok"), scatter_dimension=0, tiled=True),
        lax.psum_scatter(out_turned, ("band", "tok"), scatter_dimension=0, tiled=True),
        lax.psum_scatter(up_turned, ("band", "tok"), scatter_dimension=0, tiled=True),
        lax.psum_scatter(grad_down, ("band", "tok"), scatter_dimension=0, tiled=True),
        lax.psum_scatter(gain_one, ("band", "tok"), scatter_dimension=0, tiled=True),
        lax.psum_scatter(gain_two, ("band", "tok"), scatter_dimension=0, tiled=True),
    )
    hyper_sums = lax.psum(
        (
            grad_token,
            grad_query,
            grad_key,
            grad_value,
            grad_mix,
            grad_expand,
            grad_shrink,
            grad_first_gain,
            grad_second_gain,
            grad_gen_b,
        ),
        ("band", "tok"),
    )
    return (
        layer_out,
        pixel_grad,
        grad_gen_w,
        hyper_sums[9],
        hyper_sums[0],
        hyper_sums[1],
        hyper_sums[2],
        hyper_sums[3],
        hyper_sums[4],
        hyper_sums[5],
        hyper_sums[6],
        hyper_sums[7],
        hyper_sums[8],
        block_sums[0].T,
        block_sums[1].T,
        block_sums[2].T,
        block_sums[3],
        block_sums[4],
        block_sums[5],
    )


def solution(mesh):
    placed = (
        P("tok", None, "band", None, None),
        P(),
        P("tok", None, None),
        P("tok", "band"),
        P("tok", "band", None, None),
        P(("band", "tok"), None),
        P(),
        P(),
        P(),
        P(),
        P(),
        P(),
        P(),
        P(),
        P(),
        P(),
        P(None, "tok"),
        P(None, "tok"),
        P(None, "tok"),
        P("tok", None),
        P(),
        P(),
    )
    return jax.shard_map(
        body,
        mesh=mesh,
        in_specs=placed,
        out_specs=(
            P("tok", "band", None, None),
            P("tok", None, "band", None, None),
            P(("band", "tok"), None),
            P(),
            P(),
            P(),
            P(),
            P(),
            P(),
            P(),
            P(),
            P(),
            P(),
            P(None, ("band", "tok")),
            P(None, ("band", "tok")),
            P(None, ("band", "tok")),
            P(("band", "tok"), None),
            P(("band", "tok")),
            P(("band", "tok")),
        ),
        check_vma=False,
    )
```

profile of v0, /device:TPU:0, one launch (start us, length us, event | category | flops | bytes accessed | tf_op | source)
XLA Modules:
  0.0 2059.1 jit_solution(18307944858478254983)
XLA Ops:
  21.3 6.0 fusion.22
  30.2 259.9 %all-gather.8.cloned.1.call-done = bf16[196608,128]{1,0:T(8,128)(2,1)} async-done(((bf16[6144,128]{1,0:T(8,128)(2,1)}), bf16[196608,128]{1,0:T(8,128)(2,1)}) %all-gather.8.cloned.1.call-update) | async-done | bytes 50331664 | tf_op jit(solution)/shard_map/all_gather | solution.py:284
  290.0 25.9 %fusion.1 = bf16[32,196608]{1,0:T(8,128)(2,1)} fusion(bf16[32,128]{1,0:T(8,128)(2,1)S(1)} %bitcast.310, bf16[196608,128]{1,0:T(8,128)(2,1)} %all-gather.8.cloned.1.call-done), kind=kOutput, calls=%fused_computation.3 | convolution fusion | flops 1623195648 | bytes 62922752 | tf_op jit(solution)/shard_map/dot_general | solution.py:93
  315.9 8.2 copy.211
  333.5 69.1 %reduce-scatter.7.cloned.1.call-done = bf16[256,768]{1,0:T(8,128)(2,1)} async-done(((bf16[2048,768]{1,0:T(8,128)(2,1)}), bf16[256,768]{1,0:T(8,128)(2,1)}) %reduce-scatter.7.cloned.1.call-update) | async-done | bytes 393232 | tf_op jit(solution)/shard_map/reduce_scatter | solution.py:291
  427.7 29.5 %all-gather.16.cloned.1.call-done = bf16[3072,768]{1,0:T(8,128)(2,1)} async-done(((bf16[768,768]{1,0:T(8,128)(2,1)}), bf16[3072,768]{1,0:T(8,128)(2,1)}) %all-gather.16.cloned.1.call-update) | async-done | bytes 4718608 | tf_op jit(solution)/shard_map/all_gather | solution.py:270
  457.3 10.8 add_convert_fusion
  495.9 51.9 %all-gather.18.cloned.1.call-done = bf16[2048,768]{1,0:T(8,128)(2,1)} async-done(((bf16[256,768]{1,0:T(8,128)(2,1)}), bf16[2048,768]{1,0:T(8,128)(2,1)}) %all-gather.18.cloned.1.call-update) | async-done | bytes 3145744 | tf_op jit(solution)/shard_map/all_gather | solution.py:320
  547.8 11.1 convert_bitcast_fusion
  558.8 16.8 copy.212
  575.6 23.0 %convolution_multiply_fusion.5 = f32[32,128]{1,0:T(8,128)S(1)} fusion(bf16[32,196608]{1,0:T(8,128)(2,1)} %bitcast.272, bf16[196608,128]{1,0:T(8,128)(2,1)} %all-gather.8.cloned.1.call-done), kind=kOutput, calls=%fused_computation.123 | convolution fusion | flops 1610616832 | bytes 62930944 | tf_op jit(solution)/shard_map/dot_general | solution.py:329
  628.8 6.3 convolution_bitcast_fusion
  641.6 11.6 fusion.34
  653.9 6.6 fusion.194
  661.3 39.6 %convolution_multiply_fusion = f32[196608,128]{1,0:T(8,128)} fusion(bf16[32,196608]{1,0:T(8,128)(2,1)} %bitcast.273, bf16[32,128]{1,0:T(8,128)(2,1)S(1)} %bitcast.311), kind=kOutput, calls=%fused_computation.1 | convolution fusion | flops 1635778560 | bytes 113254400 | tf_op jit(solution)/shard_map/dot_general | solution.py:87
  710.2 13.5 fusion.65
  723.7 11.1 convert_bitcast_fusion.1
  734.9 6.6 copy.179
  745.3 39.6 %all-reduce.4 = (f32[128]{0:T(128)}, f32[128]{0:T(128)}, f32[128]{0:T(128)}, f32[768]{0:T(1024)S(1)}, f32[768]{0:T(1024)S(1)}) all-reduce(f32[128]{0:T(128)S(1)} %fusion.148, f32[128]{0:T(128)S(1)} %copy-done.107, f32[128]{0:T(128)S(1)} %copy-done.106, f32[768]{0:T(1024)S(1)} %copy-done.105, ...), channel_id=1, replica_groups=mesh['band'=8,'tok'=4] {'band','tok'}, use_global_device_ids=true, to_apply=%region_34.35 | all-reduce | flops 1920 | bytes 15360 | tf_op jit(solution)/shard_map/psum | solution.py:360
  786.1 12.8 all-reduce.8.cloned.1.call-done
  798.9 124.6 %reduce-scatter.11.cloned.1.call-done = f32[72,768]{1,0:T(8,128)} async-done(((f32[2304,768]{1,0:T(8,128)}), f32[72,768]{1,0:T(8,128)}) %reduce-scatter.11.cloned.1.call-update) | async-done | bytes 221200 | tf_op jit(solution)/shard_map/reduce_scatter | solution.py:353
  923.5 142.3 %reduce-scatter.17.cloned.1.call-done = f32[96,768]{1,0:T(8,128)} async-done(((f32[3072,768]{1,0:T(8,128)}), f32[96,768]{1,0:T(8,128)}) %reduce-scatter.17.cloned.1.call-update) | async-done | bytes 294928 | tf_op jit(solution)/shard_map/reduce_scatter | solution.py:356
  1065.8 141.0 %reduce-scatter.15.cloned.1.call-done = f32[96,768]{1,0:T(8,128)} async-done(((f32[3072,768]{1,0:T(8,128)}), f32[96,768]{1,0:T(8,128)}) %reduce-scatter.15.cloned.1.call-update) | async-done | bytes 294928 | tf_op jit(solution)/shard_map/reduce_scatter | solution.py:355
  1206.8 833.8 %reduce-scatter.9.cloned.1.call-done = f32[6144,128]{1,0:T(8,128)} async-done(((f32[196608,128]{1,0:T(8,128)}), f32[6144,128]{1,0:T(8,128)}) %reduce-scatter.9.cloned.1.call-update) | async-done | bytes 3145744 | tf_op jit(solution)/shard_map/reduce_scatter | solution.py:330
  (373 shorter events, 139.6 us)
Async XLA Ops:
  8.1 282.0 %all-gather.8.cloned.1.call-start = ((), (), s32[]{:S(2)}) async-start(), calls=%async_computation.6 | async-start | bytes 51904512 | tf_op jit(solution)/shard_map/all_gather | solution.py:284
  8.8 393.8 %reduce-scatter.7.cloned.1.call-start = ((), (), s32[]{:S(2)}) async-start(), calls=%async_computation.7 | async-start | bytes 3538944 | tf_op jit(solution)/shard_map/reduce_scatter | solution.py:291
  29.9 286.0 %copy-start.67 = (f32[8,33]{1,0:T(8,128)}, f32[8,33]{1,0:T(8,128)S(1)}, u32[]{:S(2)}) copy-start(f32[8,33]{1,0:T(8,128)S(1)} %multiply_reduce_fusion.14) | copy-start | bytes 3172
  30.2 285.8 %copy-start.57 = (bf16[8,4,128]{2,1,0:T(4,128)(2,1)}, bf16[8,4,128]{2,1,0:T(4,128)(2,1)S(1)}, u32[]{:S(2)}) copy-start(bf16[8,4,128]{2,1,0:T(4,128)(2,1)S(1)} %dynamic-slice_convert_fusion) | copy-start | bytes 24580
  329.9 76.1 %all-gather.10.cloned.1.call-start = ((), (), s32[]{:S(2)}) async-start(), calls=%async_computation.8 | async-start | bytes 4423680 | tf_op jit(solution)/shard_map/all_gather | solution.py:267
  330.5 75.6 %copy-start.69 = (f32[768]{0:T(1024)S(1)}, f32[768]{0:T(1024)}, u32[]{:S(2)}) copy-start(f32[768]{0:T(1024)} %param.42) | copy-start | bytes 9220
  330.5 88.0 %all-gather.12.cloned.1.call-start = ((), (), s32[]{:S(2)}) async-start(), calls=%async_computation.9 | async-start | bytes 1474560 | tf_op jit(solution)/shard_map/all_gather | solution.py:268
  331.1 91.2 %all-gather.14.cloned.1.call-start = ((), (), s32[]{:S(2)}) async-start(), calls=%async_computation.10 | async-start | bytes 5898240 | tf_op jit(solution)/shard_map/all_gather | solution.py:269
  331.6 125.6 %all-gather.16.cloned.1.call-start = ((), (), s32[]{:S(2)}) async-start(), calls=%async_computation.11 | async-start | bytes 5898240 | tf_op jit(solution)/shard_map/all_gather | solution.py:270
  332.4 215.4 %all-gather.18.cloned.1.call-start = ((), (), s32[]{:S(2)}) async-start(), calls=%async_computation.17 | async-start | bytes 3538944 | tf_op jit(solution)/shard_map/all_gather | solution.py:320
  332.4 73.2 %copy-start.94 = (f32[8,1,128]{2,1,0:T(1,128)}, f32[8,1,128]{2,1,0:T(1,128)S(1)}, u32[]{:S(2)}) copy-start(f32[8,1,128]{2,1,0:T(1,128)S(1)} %slice.33) | copy-start | bytes 12292
  333.1 80.0 %copy-start.95 = (pred[256]{0:T(512)(128)(4,1)}, pred[256]{0:T(512)(128)(4,1)S(1)}, u32[]{:S(2)}) copy-start(pred[256]{0:T(512)(128)(4,1)S(1)} %iota_compare_fusion.1) | copy-start | bytes 772
  333.5 76.8 %copy-start.59 = (f32[768]{0:T(1024)}, f32[768]{0:T(1024)S(1)}, u32[]{:S(2)}) copy-start(f32[768]{0:T(1024)S(1)} %convolution_reduce_fusion) | copy-start | bytes 9220
  487.1 299.0 %reduce-scatter.13.cloned.1.call-start = ((), (), s32[]{:S(2)}) async-start(), calls=%async_computation.14 | async-start | bytes 2433024 | tf_op jit(solution)/shard_map/reduce_scatter | solution.py:354
  494.3 304.5 %all-reduce.8.cloned.1.call-start = ((), (), s32[]{:S(2)}) async-start(), calls=%async_computation.18 | async-start | bytes 5505024 | tf_op jit(solution)/shard_map/psum | solution.py:360
  575.6 23.8 %copy-start.68 = (f32[8,33]{1,0:T(8,128)S(1)}, f32[8,33]{1,0:T(8,128)}, u32[]{:S(2)}) copy-start(f32[8,33]{1,0:T(8,128)} %copy-done.67) | copy-start | bytes 3172
  575.6 24.1 %copy-start.5 = (f32[8,33,2048]{2,1,0:T(8,128)S(1)}, f32[8,33,2048]{2,1,0:T(8,128)}, u32[]{:S(2)}) copy-start(f32[8,33,2048]{2,1,0:T(8,128)} %copy-done.4) | copy-start | bytes 6488068
  575.6 24.1 %copy-start.8 = (f32[8,33,2048]{2,1,0:T(8,128)S(1)}, f32[8,33,2048]{2,1,0:T(8,128)}, u32[]{:S(2)}) copy-start(f32[8,33,2048]{2,1,0:T(8,128)} %copy-done.7) | copy-start | bytes 6488068
  635.1 288.3 %reduce-scatter.11.cloned.1.call-start = ((), (), s32[]{:S(2)}) async-start(), calls=%async_computation.13 | async-start | bytes 7299072 | tf_op jit(solution)/shard_map/reduce_scatter | solution.py:353
  640.6 425.2 %reduce-scatter.17.cloned.1.call-start = ((), (), s32[]{:S(2)}) async-start(), calls=%async_computation.16 | async-start | bytes 9732096 | tf_op jit(solution)/shard_map/reduce_scatter | solution.py:356
  653.2 553.6 %reduce-scatter.15.cloned.1.call-start = ((), (), s32[]{:S(2)}) async-start(), calls=%async_computation.15 | async-start | bytes 9732096 | tf_op jit(solution)/shard_map/reduce_scatter | solution.py:355
  660.6 1380.0 %reduce-scatter.9.cloned.1.call-start = ((), (), s32[]{:S(2)}) async-start(), calls=%async_computation.12 | async-start | bytes 103809024 | tf_op jit(solution)/shard_map/reduce_scatter | solution.py:330
  742.5 1309.1 %copy-start.1 = (f32[128,2048]{1,0:T(8,128)S(1)}, f32[128,2048]{1,0:T(8,128)}, u32[]{:S(2)}) copy-start(f32[128,2048]{1,0:T(8,128)} %param.34) | copy-start | bytes 3145732
  798.9 1251.7 %copy-start.46 = (f32[2048,128]{1,0:T(8,128)S(1)}, f32[2048,128]{1,0:T(8,128)}, u32[]{:S(2)}) copy-start(f32[2048,128]{1,0:T(8,128)} %get-tuple-element.165) | copy-start | bytes 3145732
  (99 other events, 464.0 us)
Sparse Core Ops, SparseCore 0:
  11.8 278.2 all-gather.7
  330.0 72.5 reduce-scatter.6
  487.3 60.4 all-gather.17
  553.5 97.6 reduce-scatter.12
  659.7 139.0 all-reduce.7
  805.0 118.4 reduce-scatter.10
  931.0 134.7 reduce-scatter.16
  1072.3 134.5 reduce-scatter.14
  1215.0 825.6 reduce-scatter.8
Sparse Core Ops, SparseCore 1:
  331.9 28.7 all-gather.9
  362.2 17.3 all-gather.11
  381.0 37.3 all-gather.13
  419.9 37.3 all-gather.15
where the time goes:
time: 2070 us; the launch traced here: 2060 us
  waiting for transfers between devices  1670 us (81%)
  matrix products  245 us (12%)
  local copies, waits for them, and re-layouts  65.3 us (3%)
  blocking collectives  39.6 us (2%)
  other arithmetic  22.8 us (1%)
    reduce_scatter x1, waiting for transfers between devices, body(): lax.psum_scatter(contract_rows(d_kernel, band_low) * factor, ('band', 'to...  834 us
    all_gather x1, waiting for transfers between devices, body(): gen_full = lax.all_gather(gen_w, ('band', 'tok'), axis=0, tiled=True)  260 us
    reduce_scatter x1, waiting for transfers between devices, body(): lax.psum_scatter(grad_down, ('band', 'tok'), scatter_dimension=0, tiled=T...  142 us
    reduce_scatter x1, waiting for transfers between devices, body(): lax.psum_scatter(up_turned, ('band', 'tok'), scatter_dimension=0, tiled=T...  141 us
    reduce_scatter x1, waiting for transfers between devices, body(): lax.psum_scatter(qkv_turned, ('band', 'tok'), scatter_dimension=0, tiled=...  125 us
    reduce_scatter x1, waiting for transfers between devices, body(): lax.psum_scatter(product.reshape(own_images * slot_count * lax.axis_size(...  69.1 us
    dot_general x5, matrix products, contract_rows(): lax.dot_general(left_side, right_side, (((0,), (0,)), ((), ())), preferre...  66.2 us
    unnamed x232, local copies, waits for them, and re-layouts  54.6 us
  transfers between devices with their start and end apart: 13, of which 9 were waited for; matrix products, arithmetic and copies ran while one was open for 12% of the time, Pallas kernels for 0%

commit v1 on v0

--- a/solution.py
+++ b/solution.py
@@ -317,7 +317,23 @@
     d_bias = jnp.sum(d_embed.reshape(own_images, slot_count, model_dim), axis=1)
     d_bias_feat = jnp.dot(d_bias, gen_b.T, precision=PRECISE)
     grad_gen_b = jnp.dot(bias_own.T, d_bias, precision=PRECISE)
-    d_gathered = lax.all_gather(d_embed_low, "band", axis=0, tiled=True)
+    ways, here, hop = (lax.axis_size("band"), lax.axis_index("band"), d_embed_low.shape[0])
+    dims = [n * ways if d == 0 else n for d, n in enumerate(d_embed_low.shape)]
+    full = lax.dynamic_update_slice_in_dim(
+        jnp.zeros(dims, d_embed_low.dtype), d_embed_low, here * hop, axis=0
+    )
+    going_up = going_down = d_embed_low
+    for far in range(1, ways // 2 + 1):
+        going_up = lax.ppermute(going_up, "band", [(d, (d + 1) % ways) for d in range(ways)])
+        full = lax.dynamic_update_slice_in_dim(full, going_up, (here - far) % ways * hop, axis=0)
+        if 2 * far < ways:
+            going_down = lax.ppermute(
+                going_down, "band", [(d, (d - 1) % ways) for d in range(ways)]
+            )
+            full = lax.dynamic_update_slice_in_dim(
+                full, going_down, (here + far) % ways * hop, axis=0
+            )
+    d_gathered = full
     pixel_grad = jnp.einsum(
         "isd,ibpd->ibsp", d_gathered, kernel_grid, preferred_element_type=jnp.float32
     ).astype(jnp.bfloat16)[None]

time: 2070 us -> 2170 us (1.048)
  waiting for transfers between devices: 1670 us -> 1720 us
  local copies, waits for them, and re-layouts: 65.3 us -> 95.2 us
    reduce_scatter x1, waiting for transfers between devices: 0.01 us -> 92.9 us  [body(): lax.psum_scatter(out_turned, ('band', 'tok'), scatter_dimension=0, tiled=...]
    all_gather x1 -> x0, waiting for transfers between devices: 51.9 us -> none  [body(): d_gathered = lax.all_gather(d_embed_low, 'band', axis=0, tiled=True)]
    ppermute x0 -> x7, waiting for transfers between devices: none -> 25.2 us  [the longest x4 25.2 us: body(): lax.ppermute(going_up, 'band', [(d, (d + 1) % ways) for d in range(ways)])]
    unnamed x232 -> x226, local copies, waits for them, and re-layouts: 54.6 us -> 52.4 us
  transfers between devices with their start and end apart: 13 -> 19, of which waited for: 9 -> 10; matrix products, arithmetic and copies ran while one was open for 12% -> 9% of each run, Pallas kernels for 0% -> 0%
where the time goes in v1:
time: 2170 us; the launch traced here: 2160 us
  waiting for transfers between devices  1720 us (79%)
  matrix products  242 us (11%)
  local copies, waits for them, and re-layouts  95.2 us (4%)
  blocking collectives  39.7 us (2%)
  other arithmetic  23.4 us (1%)
    reduce_scatter x1, waiting for transfers between devices, body(): lax.psum_scatter(contract_rows(d_kernel, band_low) * factor, ('band', 'to...  834 us
    all_gather x1, waiting for transfers between devices, body(): gen_full = lax.all_gather(gen_w, ('band', 'tok'), axis=0, tiled=True)  260 us
    reduce_scatter x1, waiting for transfers between devices, body(): lax.psum_scatter(grad_down, ('band', 'tok'), scatter_dimension=0, tiled=T...  142 us
    reduce_scatter x1, waiting for transfers between devices, body(): lax.psum_scatter(up_turned, ('band', 'tok'), scatter_dimension=0, tiled=T...  141 us
    reduce_scatter x1, waiting for transfers between devices, body(): lax.psum_scatter(qkv_turned, ('band', 'tok'), scatter_dimension=0, tiled=...  124 us
    reduce_scatter x1, waiting for transfers between devices, body(): lax.psum_scatter(out_turned, ('band', 'tok'), scatter_dimension=0, tiled=...  92.9 us
    reduce_scatter x1, waiting for transfers between devices, body(): lax.psum_scatter(product.reshape(own_images * slot_count * lax.axis_size(...  69.3 us
    dot_general x5, matrix products, contract_rows(): lax.dot_general(left_side, right_side, (((0,), (0,)), ((), ())), preferre...  64.8 us
  transfers between devices with their start and end apart: 19, of which 10 were waited for; matrix products, arithmetic and copies ran while one was open for 9% of the time, Pallas kernels for 0%

profile of v1, /device:TPU:0, one launch (start us, length us, event | category | flops | bytes accessed | tf_op | source)
XLA Modules:
  0.0 2155.9 jit_solution(16485216137974787060)
XLA Ops:
  30.2 259.9 %all-gather.6.cloned.1.call-done = bf16[196608,128]{1,0:T(8,128)(2,1)} async-done(((bf16[6144,128]{1,0:T(8,128)(2,1)}), bf16[196608,128]{1,0:T(8,128)(2,1)}) %all-gather.6.cloned.1.call-update) | async-done | bytes 50331664 | tf_op jit(solution)/shard_map/all_gather | solution.py:284
  290.0 25.9 %fusion.1 = bf16[32,196608]{1,0:T(8,128)(2,1)} fusion(bf16[32,128]{1,0:T(8,128)(2,1)S(1)} %bitcast.313, bf16[196608,128]{1,0:T(8,128)(2,1)} %all-gather.6.cloned.1.call-done), kind=kOutput, calls=%fused_computation.3 | convolution fusion | flops 1623195648 | bytes 62922752 | tf_op jit(solution)/shard_map/dot_general | solution.py:93
  315.9 8.2 copy.243
  333.5 69.3 %reduce-scatter.7.cloned.1.call-done = bf16[256,768]{1,0:T(8,128)(2,1)} async-done(((bf16[2048,768]{1,0:T(8,128)(2,1)}), bf16[256,768]{1,0:T(8,128)(2,1)}) %reduce-scatter.7.cloned.1.call-update) | async-done | bytes 393232 | tf_op jit(solution)/shard_map/reduce_scatter | solution.py:291
  427.8 29.4 %all-gather.14.cloned.1.call-done = bf16[3072,768]{1,0:T(8,128)(2,1)} async-done(((bf16[768,768]{1,0:T(8,128)(2,1)}), bf16[3072,768]{1,0:T(8,128)(2,1)}) %all-gather.14.cloned.1.call-update) | async-done | bytes 4718608 | tf_op jit(solution)/shard_map/all_gather | solution.py:270
  457.3 10.7 add_convert_fusion
  491.8 14.3 collective-permute-done
  514.4 10.9 collective-permute-done.2
  563.7 11.1 convert_bitcast_fusion
  574.7 16.6 copy.244
  591.4 22.4 %convolution_multiply_fusion.5 = f32[32,128]{1,0:T(8,128)S(1)} fusion(bf16[32,196608]{1,0:T(8,128)(2,1)} %bitcast.277, bf16[196608,128]{1,0:T(8,128)(2,1)} %all-gather.6.cloned.1.call-done), kind=kOutput, calls=%fused_computation.126 | convolution fusion | flops 1610616832 | bytes 62930944 | tf_op jit(solution)/shard_map/dot_general | solution.py:345
  616.3 6.3 convolution_bitcast_fusion
  658.5 11.6 fusion.39
  670.8 6.7 fusion.199
  678.2 39.2 %convolution_multiply_fusion = f32[196608,128]{1,0:T(8,128)} fusion(bf16[32,196608]{1,0:T(8,128)(2,1)} %bitcast.278, bf16[32,128]{1,0:T(8,128)(2,1)S(1)} %bitcast.314), kind=kOutput, calls=%fused_computation.1 | convolution fusion | flops 1635778560 | bytes 113254400 | tf_op jit(solution)/shard_map/dot_general | solution.py:87
  726.8 13.5 fusion.70
  740.3 11.3 convert_bitcast_fusion.1
  751.7 6.6 copy.211
  762.0 39.7 %all-reduce.4 = (f32[128]{0:T(128)}, f32[128]{0:T(128)}, f32[128]{0:T(128)}, f32[768]{0:T(1024)S(1)}, f32[768]{0:T(1024)S(1)}) all-reduce(f32[128]{0:T(128)S(1)} %fusion.153, f32[128]{0:T(128)S(1)} %copy-done.104, f32[128]{0:T(128)S(1)} %copy-done.103, f32[768]{0:T(1024)S(1)} %copy-done.102, ...), channel_id=1, replica_groups=mesh['band'=8,'tok'=4] {'band','tok'}, use_global_device_ids=true, to_apply=%region_34.35 | all-reduce | flops 1920 | bytes 15360 | tf_op jit(solution)/shard_map/psum | solution.py:376
  802.9 92.9 %reduce-scatter.13.cloned.1.call-done = f32[24,768]{1,0:T(8,128)} async-done(((f32[768,768]{1,0:T(8,128)}), f32[24,768]{1,0:T(8,128)}) %reduce-scatter.13.cloned.1.call-update) | async-done | bytes 73744 | tf_op jit(solution)/shard_map/reduce_scatter | solution.py:370
  895.8 124.2 %reduce-scatter.11.cloned.1.call-done = f32[72,768]{1,0:T(8,128)} async-done(((f32[2304,768]{1,0:T(8,128)}), f32[72,768]{1,0:T(8,128)}) %reduce-scatter.11.cloned.1.call-update) | async-done | bytes 221200 | tf_op jit(solution)/shard_map/reduce_scatter | solution.py:369
  1020.0 142.3 %reduce-scatter.17.cloned.1.call-done = f32[96,768]{1,0:T(8,128)} async-done(((f32[3072,768]{1,0:T(8,128)}), f32[96,768]{1,0:T(8,128)}) %reduce-scatter.17.cloned.1.call-update) | async-done | bytes 294928 | tf_op jit(solution)/shard_map/reduce_scatter | solution.py:372
  1162.2 141.1 %reduce-scatter.15.cloned.1.call-done = f32[96,768]{1,0:T(8,128)} async-done(((f32[3072,768]{1,0:T(8,128)}), f32[96,768]{1,0:T(8,128)}) %reduce-scatter.15.cloned.1.call-update) | async-done | bytes 294928 | tf_op jit(solution)/shard_map/reduce_scatter | solution.py:371
  1303.3 833.9 %reduce-scatter.9.cloned.1.call-done = f32[6144,128]{1,0:T(8,128)} async-done(((f32[196608,128]{1,0:T(8,128)}), f32[6144,128]{1,0:T(8,128)}) %reduce-scatter.9.cloned.1.call-update) | async-done | bytes 3145744 | tf_op jit(solution)/shard_map/reduce_scatter | solution.py:346
  (395 shorter events, 189.7 us)
Async XLA Ops:
  8.1 282.0 %all-gather.6.cloned.1.call-start = ((), (), s32[]{:S(2)}) async-start(), calls=%async_computation.6 | async-start | bytes 51904512 | tf_op jit(solution)/shard_map/all_gather | solution.py:284
  8.8 394.0 %reduce-scatter.7.cloned.1.call-start = ((), (), s32[]{:S(2)}) async-start(), calls=%async_computation.7 | async-start | bytes 3538944 | tf_op jit(solution)/shard_map/reduce_scatter | solution.py:291
  29.9 286.0 %copy-start.65 = (f32[8,33]{1,0:T(8,128)}, f32[8,33]{1,0:T(8,128)S(1)}, u32[]{:S(2)}) copy-start(f32[8,33]{1,0:T(8,128)S(1)} %multiply_reduce_fusion.14) | copy-start | bytes 3172
  30.2 285.8 %copy-start.54 = (bf16[8,4,128]{2,1,0:T(4,128)(2,1)}, bf16[8,4,128]{2,1,0:T(4,128)(2,1)S(1)}, u32[]{:S(2)}) copy-start(bf16[8,4,128]{2,1,0:T(4,128)(2,1)S(1)} %dynamic-slice_convert_fusion) | copy-start | bytes 24580
  329.9 76.3 %all-gather.8.cloned.1.call-start = ((), (), s32[]{:S(2)}) async-start(), calls=%async_computation.8 | async-start | bytes 4423680 | tf_op jit(solution)/shard_map/all_gather | solution.py:267
  330.5 88.1 %all-gather.10.cloned.1.call-start = ((), (), s32[]{:S(2)}) async-start(), calls=%async_computation.9 | async-start | bytes 1474560 | tf_op jit(solution)/shard_map/all_gather | solution.py:268
  331.1 91.3 %all-gather.12.cloned.1.call-start = ((), (), s32[]{:S(2)}) async-start(), calls=%async_computation.10 | async-start | bytes 5898240 | tf_op jit(solution)/shard_map/all_gather | solution.py:269
  331.6 125.6 %all-gather.14.cloned.1.call-start = ((), (), s32[]{:S(2)}) async-start(), calls=%async_computation.11 | async-start | bytes 5898240 | tf_op jit(solution)/shard_map/all_gather | solution.py:270
  332.4 470.5 %all-reduce.8.cloned.1.call-start = ((), (), s32[]{:S(2)}) async-start(), calls=%async_computation.17 | async-start | bytes 5505024 | tf_op jit(solution)/shard_map/psum | solution.py:376
  333.1 80.1 %copy-start.92 = (pred[256]{0:T(512)(128)(4,1)}, pred[256]{0:T(512)(128)(4,1)S(1)}, u32[]{:S(2)}) copy-start(pred[256]{0:T(512)(128)(4,1)S(1)} %iota_compare_fusion.1) | copy-start | bytes 772
  487.1 19.0 collective-permute-start
  488.6 20.8 collective-permute-start.1
  506.1 19.2 collective-permute-start.2
  509.4 27.4 %collective-permute-start.3 = (bf16[1,256,768]{2,1,0:T(8,128)(2,1)}, bf16[1,256,768]{2,1,0:T(8,128)(2,1)}, u32[]{:S(2)}, u32[]{:S(2)}) collective-permute-start(bf16[1,256,768]{2,1,0:T(8,128)(2,1)} %collective-permute-done.1), channel_id=1, source_target_pairs={{0,28},{4,0},{8,4},{12,8},{16,12},{20,16},{24,20},{28,24},{1,29},{... | collective-permute-start | bytes 1179656 | tf_op jit(solution)/shard_map/ppermute | solution.py:330
  525.3 21.6 %collective-permute-start.4 = (bf16[1,256,768]{2,1,0:T(8,128)(2,1)}, bf16[1,256,768]{2,1,0:T(8,128)(2,1)}, u32[]{:S(2)}, u32[]{:S(2)}) collective-permute-start(bf16[1,256,768]{2,1,0:T(8,128)(2,1)} %collective-permute-done.2), channel_id=1, source_target_pairs={{0,4},{4,8},{8,12},{12,16},{16,20},{20,24},{24,28},{28,0},{1,5},{5... | collective-permute-start | bytes 1179656 | tf_op jit(solution)/shard_map/ppermute | solution.py:327
  536.8 17.7 collective-permute-start.5
  547.0 13.0 collective-permute-start.6
  649.8 245.9 %reduce-scatter.13.cloned.1.call-start = ((), (), s32[]{:S(2)}) async-start(), calls=%async_computation.14 | async-start | bytes 2433024 | tf_op jit(solution)/shard_map/reduce_scatter | solution.py:370
  651.8 368.1 %reduce-scatter.11.cloned.1.call-start = ((), (), s32[]{:S(2)}) async-start(), calls=%async_computation.13 | async-start | bytes 7299072 | tf_op jit(solution)/shard_map/reduce_scatter | solution.py:369
  657.5 504.7 %reduce-scatter.17.cloned.1.call-start = ((), (), s32[]{:S(2)}) async-start(), calls=%async_computation.16 | async-start | bytes 9732096 | tf_op jit(solution)/shard_map/reduce_scatter | solution.py:372
  670.2 633.1 %reduce-scatter.15.cloned.1.call-start = ((), (), s32[]{:S(2)}) async-start(), calls=%async_computation.15 | async-start | bytes 9732096 | tf_op jit(solution)/shard_map/reduce_scatter | solution.py:371
  677.5 1459.7 %reduce-scatter.9.cloned.1.call-start = ((), (), s32[]{:S(2)}) async-start(), calls=%async_computation.12 | async-start | bytes 103809024 | tf_op jit(solution)/shard_map/reduce_scatter | solution.py:346
  759.2 1388.9 %copy-start.1 = (f32[128,2048]{1,0:T(8,128)S(1)}, f32[128,2048]{1,0:T(8,128)}, u32[]{:S(2)}) copy-start(f32[128,2048]{1,0:T(8,128)} %param.34) | copy-start | bytes 3145732
  802.9 1344.2 %copy-start.42 = (f32[2048,128]{1,0:T(8,128)S(1)}, f32[2048,128]{1,0:T(8,128)}, u32[]{:S(2)}) copy-start(f32[2048,128]{1,0:T(8,128)} %get-tuple-element.165) | copy-start | bytes 3145732
  (102 other events, 753.4 us)
Sparse Core Ops, SparseCore 0:
  11.8 278.2 all-gather.5
  330.0 72.7 reduce-scatter.6
  649.9 140.9 all-reduce.7
  797.5 98.2 reduce-scatter.12
  901.9 118.0 reduce-scatter.10
  1027.3 134.8 reduce-scatter.16
  1168.7 134.5 reduce-scatter.14
  1311.4 825.6 reduce-scatter.8
Sparse Core Ops, SparseCore 1:
  331.9 28.7 all-gather.7
  362.2 17.3 all-gather.9
  381.0 37.3 all-gather.11
  419.9 37.3 all-gather.13
